TPU v7x, 32 devices: a whole 2x2x4 slice. The times are simulated.
32 devices in a mesh: dp: 8 (over y, x, core), fsdp: 4 (over z).
Axes of the slice: x: 2, y: 2, z: 4, core: 2. Of those that a mesh axis runs over, the one named last changes fastest.
Arguments:
- img_emb: bfloat16 [1024, 1024], P(('dp', 'fsdp')), may hold values from -0.25 to 0.25
- txt_emb: bfloat16 [1024, 1024], P(('dp', 'fsdp')), may hold values from -0.25 to 0.25
- img_ids: int32 [1024], P(('dp', 'fsdp')), may hold values from 0 to 1023
- txt_ids: int32 [1024], P(('dp', 'fsdp')), may hold values from 0 to 1023
- temp_log: float32 [1], replicated, may hold values from 1.5 to 2.5
- logit_bias: float32 [1], replicated, may hold values from -6 to -2
- block_in: bfloat16 [2048, 3072], P(('dp', 'fsdp')), may hold values from -6 to 6
- dw_kernel: float32 [49, 3072], replicated, may hold values from -0.875 to 0.875
- ln_gain: float32 [3072], replicated, may hold values from 0.5 to 1.5
- ln_bias: float32 [3072], replicated, may hold values from -3 to 3
- w_up: bfloat16 [3072, 6144], P(None, 'fsdp'), may hold values from -0.109375 to 0.109375
- w_down: bfloat16 [6144, 3072], P('fsdp'), may hold values from -0.078125 to 0.078125
- layer_scale: float32 [3072], replicated, may hold values from 0.1 to 1
- head_gain: float32 [3072], replicated, may hold values from 0.5 to 1.5
- head_bias: float32 [3072], replicated, may hold values from -3 to 3
- w_proj: bfloat16 [3072, 1024], replicated, may hold values from -0.109375 to 0.109375
Outputs:
- img_grad: float32 [1024, 1024], P(('dp', 'fsdp'))
- txt_grad: float32 [1024, 1024], P(('dp', 'fsdp'))
- w_up_grad: float32 [3072, 6144], P('dp', 'fsdp')
- w_down_grad: float32 [6144, 3072], P('fsdp', 'dp')
All inputs are finite; a program needn't handle non-finite values.
Results may differ from a plain program's by a relative error of at most 0.02.
Values may be sent and summed in bfloat16 or wider, within the bound.
A program may use at most 128 MiB of HBM per device.

v0:
```python
import jax
import jax.numpy as jnp
from jax import lax
from jax.sharding import PartitionSpec as P

KERNEL = 7
SIDE = 8


def unit_rows(matrix):
    values = matrix.astype(jnp.float32)
    length = jnp.sqrt(jnp.sum(values * values, axis=1, keepdims=True) + 1e-06)
    return (values / length, length)


def back_unit(gradient, unit_part, length):
    inner_prod = jnp.sum(unit_part * gradient, axis=1, keepdims=True)
    return (gradient - unit_part * inner_prod) / length


def depthwise(pictures, kernel):
    reach = KERNEL // 2
    padded = jnp.pad(pictures, ((0, 0), (reach, reach), (reach, reach), (0, 0)))
    summed = jnp.zeros_like(pictures)
    for above in range(KERNEL):
        for across in range(KERNEL):
            summed = (
                summed
                + kernel[above * KERNEL + across]
                * padded[:, above : above + SIDE, across : across + SIDE, :]
            )
    return summed


def layer_norm(values, gain_vec, bias_vec):
    centre = jnp.mean(values, axis=-1, keepdims=True)
    centred = values - centre
    inverse = 1.0 / jnp.sqrt(jnp.mean(centred * centred, axis=-1, keepdims=True) + 1e-06)
    normal = centred * inverse
    return (normal * gain_vec + bias_vec, normal, inverse)


def head_back(patch_means, block_mean, image_sum, layer_scale, head_gain, head_bias, w_proj):
    pooled = patch_means.astype(jnp.float32) + layer_scale * block_mean
    head_out, head_norm, inverse = layer_norm(pooled, head_gain, head_bias)
    embed = jnp.dot(head_out.astype(jnp.bfloat16), w_proj, preferred_element_type=jnp.float32)
    embed_unit, embed_len = unit_rows(embed)
    embed_grad = back_unit(image_sum, embed_unit, embed_len).astype(jnp.bfloat16)
    head_grad = jnp.dot(embed_grad, w_proj.T, preferred_element_type=jnp.float32)
    norm_grad = head_grad * head_gain
    pool_grad = inverse * (
        norm_grad
        - jnp.mean(norm_grad, axis=1, keepdims=True)
        - head_norm * jnp.mean(norm_grad * head_norm, axis=1, keepdims=True)
    )
    return (layer_scale * pool_grad / (SIDE * SIDE)).astype(jnp.bfloat16)


def id_columns(ids):
    codes = jnp.stack([ids // 256, ids % 256], axis=1).astype(jnp.bfloat16)
    return jnp.pad(codes, ((0, 0), (0, 126)))


def split_two(values):
    high = lax.reduce_precision(values, 8, 7)
    low = values - high
    return (high.astype(jnp.bfloat16), low.astype(jnp.bfloat16))


def pair_tile_coded(images, image_codes, text_rows, text_codes, temper, offset):
    scores = jnp.dot(images, text_rows.T, preferred_element_type=jnp.float32)
    logits = temper * scores + offset
    same = (image_codes[:, 0][:, None] == text_codes[:, 0][None, :]) & (
        image_codes[:, 1][:, None] == text_codes[:, 1][None, :]
    )
    labels = jnp.where(same, 1.0, -1.0)
    weights = (temper * -labels * jax.nn.sigmoid(-labels * logits)).astype(jnp.bfloat16)
    image_part = jnp.dot(weights, text_rows, preferred_element_type=jnp.float32)
    text_part = jnp.dot(weights.T, images, preferred_element_type=jnp.float32)
    return (image_part, text_part)


def on_device(
    img_emb,
    txt_emb,
    img_ids,
    txt_ids,
    temp_log,
    logit_bias,
    block_in,
    dw_kernel,
    ln_gain,
    ln_bias,
    w_up,
    w_down,
    layer_scale,
    head_gain,
    head_bias,
    w_proj,
):
    channels = block_in.shape[1]
    hid_width = w_up.shape[1]
    embed_width = img_emb.shape[1]
    pairs = img_emb.shape[0]
    patches = SIDE * SIDE
    n_dp, n_fsdp = (lax.axis_size("dp"), lax.axis_size("fsdp"))
    temper = jnp.exp(temp_log[0])
    offset = logit_bias[0]
    img_unit, img_len = unit_rows(img_emb)
    txt_unit, txt_len = unit_rows(txt_emb)
    img_b = jnp.concatenate([img_unit.astype(jnp.bfloat16), id_columns(img_ids)], axis=1)
    txt_b = jnp.concatenate([txt_unit.astype(jnp.bfloat16), id_columns(txt_ids)], axis=1)
    group_img = lax.all_gather(img_b, "fsdp", axis=0, tiled=True)
    column_txt = lax.all_gather(txt_b, "dp", axis=0, tiled=True)
    pictures = block_in.astype(jnp.float32).reshape(1, SIDE, SIDE, channels)
    mixed_rows = depthwise(pictures, dw_kernel).reshape(patches, channels)
    normed = layer_norm(mixed_rows, ln_gain, ln_bias)[0].astype(jnp.bfloat16)
    patch_means = jnp.mean(pictures, axis=(1, 2)).astype(jnp.bfloat16)
    group_normed = lax.all_gather(normed, "fsdp", axis=0, tiled=True)
    image_part, text_part = pair_tile_coded(
        group_img[:, :embed_width],
        group_img[:, embed_width:],
        column_txt[:, :embed_width],
        column_txt[:, embed_width:],
        temper,
        offset,
    )
    hidden = jnp.dot(group_normed, w_up, preferred_element_type=jnp.float32)
    activated, pullback = jax.vjp(jax.nn.gelu, hidden)
    slope = pullback(jnp.ones_like(hidden))[0].astype(jnp.bfloat16)
    active_total = jnp.sum(
        activated.astype(jnp.bfloat16).astype(jnp.float32).reshape(n_fsdp, patches, hid_width),
        axis=1,
    )
    high, low = split_two(active_total / patches)
    both = jnp.dot(jnp.concatenate([high, low]), w_down, preferred_element_type=jnp.float32)
    partial_mean = both[:n_fsdp] + both[n_fsdp:]
    mean_rows = channels // embed_width
    fill = -(pairs + mean_rows) % 16
    terms = jnp.concatenate(
        [
            image_part.astype(jnp.bfloat16).reshape(n_fsdp, pairs, embed_width),
            partial_mean.astype(jnp.bfloat16).reshape(n_fsdp, mean_rows, embed_width),
            jnp.zeros((n_fsdp, fill, embed_width), jnp.bfloat16),
        ],
        axis=1,
    ).reshape(-1, embed_width)
    term_sum = lax.psum_scatter(terms, "fsdp", scatter_dimension=0, tiled=True).astype(jnp.float32)
    image_sum = term_sum[:pairs]
    block_mean = term_sum[pairs : pairs + mean_rows].reshape(1, channels)
    all_slope = lax.all_gather(slope, "dp", axis=0, tiled=True)
    own_normed = lax.all_to_all(group_normed, "dp", split_axis=1, concat_axis=0, tiled=True)
    all_active = lax.all_gather(active_total, "dp", axis=0, tiled=True)
    grad_row = head_back(
        patch_means, block_mean, image_sum[:1], layer_scale, head_gain, head_bias, w_proj
    )
    all_grad = lax.all_gather(grad_row, ("dp", "fsdp"), axis=0, tiled=True)
    row_down = jnp.dot(all_grad, w_down.T, preferred_element_type=jnp.float32)
    hid_grad = (
        (
            all_slope.reshape(n_dp * n_fsdp, patches, hid_width).astype(jnp.float32)
            * row_down[:, None, :]
        )
        .astype(jnp.bfloat16)
        .reshape(-1, hid_width)
    )
    w_up_grad = lax.dot_general(
        own_normed, hid_grad, (((0,), (0,)), ((), ())), preferred_element_type=jnp.float32
    )
    share = channels // n_dp
    own_grad = lax.dynamic_slice_in_dim(all_grad, lax.axis_index("dp") * share, share, 1)
    high, low = split_two(all_active)
    w_down_grad = lax.dot_general(
        jnp.concatenate([high, low]),
        jnp.concatenate([own_grad, own_grad]),
        (((0,), (0,)), ((), ())),
        preferred_element_type=jnp.float32,
    )
    text_sum = lax.psum_scatter(
        text_part.astype(jnp.bfloat16), "dp", scatter_dimension=0, tiled=True
    ).astype(jnp.float32)
    img_grad = back_unit(image_sum, img_unit, img_len)
    txt_grad = back_unit(text_sum, txt_unit, txt_len)
    return (img_grad, txt_grad, w_up_grad, w_down_grad)


def solution(mesh):
    in_specs = (
        P(("dp", "fsdp"), None),
        P(("dp", "fsdp"), None),
        P(("dp", "fsdp")),
        P(("dp", "fsdp")),
        P(),
        P(),
        P(("dp", "fsdp"), None),
        P(),
        P(),
        P(),
        P(None, "fsdp"),
        P("fsdp", None),
        P(),
        P(),
        P(),
        P(),
    )
    out_specs = (P(("dp", "fsdp"), None), P(("dp", "fsdp"), None), P("dp", "fsdp"), P("fsdp", "dp"))
    return jax.shard_map(
        on_device, mesh=mesh, in_specs=in_specs, out_specs=out_specs, check_vma=False
    )
```

profile of v0, /device:TPU:0, one launch (start us, length us, event | category | flops | bytes accessed | tf_op | source)
XLA Modules:
  0.0 232.2 jit_solution(10827086138796158804)
XLA Ops:
  8.0 1.5 fusion.163
  9.5 2.1 fusion.161
  11.6 1.9 fusion.162
  13.5 1.1 convert_bitcast_fusion
  14.6 5.5 %fusion.159 = (f32[8,8]{1,0:T(8,128)S(1)}, f32[1,8,8,3072]{3,2,1,0:T(8,128)S(1)}) fusion(f32[3072]{0:T(1024)S(1)} %bitcast.123, f32[3072]{0:T(1024)S(1)} %bitcast.124, f32[3072]{0:T(1024)S(1)} %bitcast.127, f32[3072]{0:T(1024)S(1)} %bitcast.128, f32[3072]{0:T(1024)S(1)} %bitcast.129, f32[3072]{0:T(1024)S(1)} %bitcast.130, f32[3072]{0:T(1024)S(1)} %bitcast.131, ...), kind=kLoop, calls=%fused_computation.268 | loop fusion | flops 19267520 | bytes 2175232 | tf_op jit(solution)/shard_map/reduce_sum | solution.py:36
  20.2 0.2 multiply_reduce_fusion
  20.6 0.9 fusion.115
  22.9 0.1 fusion.127
  23.1 0.1 copy.41
  23.2 0.1 copy.45
  23.5 17.6 %all_gather.18 = bf16[128,1152]{1,0:T(8,128)(2,1)S(1)} all-gather(bf16[32,1152]{1,0:T(8,128)(2,1)S(1)} %fusion.131), channel_id=1, replica_groups=mesh['dp'=8,'fsdp'=4] {'fsdp'}, dimensions={0}, use_global_device_ids=true | all-gather | bytes 368640 | tf_op jit(solution)/shard_map/all_gather | solution.py:113
  41.1 0.2 slice_reduce_fusion.3
  41.2 0.1 fusion.128
  41.4 0.1 fusion.156
  41.5 10.1 %all_gather.19 = bf16[256,1152]{1,0:T(8,128)(2,1)S(1)} all-gather(bf16[32,1152]{1,0:T(8,128)(2,1)S(1)} %fusion.132), channel_id=1, replica_groups=mesh['dp'=8,'fsdp'=4] {'dp'}, dimensions={0}, use_global_device_ids=true | all-gather | bytes 663552 | tf_op jit(solution)/shard_map/all_gather | solution.py:114
  51.6 0.2 slice_reduce_fusion.1
  51.8 0.3 fusion.15
  52.1 1.1 convolution_convert_fusion
  53.3 0.2 convolution_convert_fusion.1
  53.6 9.8 %all-gather.5.cloned.1.call-done = bf16[256,3072]{1,0:T(8,128)(2,1)} async-done(((bf16[64,3072]{1,0:T(8,128)(2,1)}), bf16[256,3072]{1,0:T(8,128)(2,1)}) %all-gather.5.cloned.1.call-update) | async-done | bytes 1572880 | tf_op jit(solution)/shard_map/all_gather | solution.py:119
  63.4 6.0 %convert_reduce_fusion = (f32[4,1536]{1,0:T(4,128)S(1)}, f32[256,1536]{1,0:T(8,128)S(1)}) fusion(bf16[256,3072]{1,0:T(8,128)(2,1)} %all-gather.5.cloned.1.call-done, bf16[3072,1536]{1,0:T(8,128)(2,1)} %param.26), kind=kOutput, calls=%fused_computation.59 | convolution fusion | flops 2420238336 | bytes 12607488 | tf_op jit(solution)/shard_map/dot_general | solution.py:128
  69.4 0.6 copy-done.6
  70.0 5.0 %fusion.138 = f32[8,3072]{1,0:T(8,128)S(1)} fusion(bf16[1536,3072]{1,0:T(8,128)(2,1)} %param.27, bf16[4,1536]{1,0:T(4,128)(2,1)S(1)} %get-tuple-element.67, bf16[4,1536]{1,0:T(4,128)(2,1)S(1)} %get-tuple-element.66), kind=kOutput, calls=%fused_computation.217 | convolution fusion | flops 75546624 | bytes 9560064 | tf_op jit(solution)/shard_map/dot_general | solution.py:136
  75.1 0.9 maximum_maximum_fusion
  76.0 1.9 fusion.7
  78.0 9.9 %reduce-scatter.5.cloned.1.call-done = bf16[32,1024]{1,0:T(8,128)(2,1)} async-done(((bf16[256,1024]{1,0:T(8,128)(2,1)}), bf16[32,1024]{1,0:T(8,128)(2,1)}) %reduce-scatter.5.cloned.1.call-update) | async-done | bytes 65552 | tf_op jit(solution)/shard_map/reduce_scatter | solution.py:179
  87.9 1.1 fusion.129
  89.0 1.6 fusion.130
  90.6 1.6 copy.43
  92.2 3.7 %all-to-all-start = ((bf16[256,8,384]{0,2,1:T(8,128)(2,1)}), bf16[256,8,384]{0,2,1:T(8,128)(2,1)S(1)}, u32[]{:S(2)}, u32[]{:S(2)}) async-start(bf16[256,8,384]{0,2,1:T(8,128)(2,1)} %bitcast.61), calls=%async_computation.2 | async-start | bytes 3145728 | tf_op jit(solution)/shard_map/all_to_all | solution.py:152
  95.9 24.4 %all-gather.1 = f32[8,4,1536]{2,1,0:T(4,128)S(1)} all-gather(f32[1,4,1536]{2,1,0:T(4,128)S(1)} %bitcast.109), channel_id=1, replica_groups=mesh['dp'=8,'fsdp'=4] {'dp'}, dimensions={0}, use_global_device_ids=true | all-gather | bytes 221184 | tf_op jit(solution)/shard_map/all_gather | solution.py:153
  120.5 0.7 slice.449
  121.3 0.6 fusion.158
  122.5 0.6 multiply_reduce_fusion.3
  123.9 3.7 %fusion.164 = f32[1,1024]{1,0:T(1,128)S(1)} fusion(bf16[3072,1]{0,1:T(2,128)(2,1)S(1)} %reshape.344, bf16[3072,1024]{1,0:T(8,128)(2,1)} %param.31), kind=kOutput, calls=%fused_computation.272 | convolution fusion | flops 6291456 | bytes 6301696 | tf_op jit(solution)/shard_map/dot_general | solution.py:46
  127.6 0.6 multiply_reduce_fusion.5
  129.0 0.6 multiply_reduce_fusion.4
  129.6 0.6 broadcast_multiply_fusion
  130.2 4.5 %fusion.142 = f32[1,3072]{1,0:T(1,128)S(1)} fusion(bf16[3072,1024]{1,0:T(8,128)(2,1)} %param.31, f32[1,1024]{1,0:T(1,128)S(1)} %bitcast.164, f32[48,1024]{1,0:T(8,128)S(1)} %convert_element_type.103, f32[]{:T(128)S(6)} %sqrt.33), kind=kOutput, calls=%fused_computation.228 | convolution fusion | flops 6294528 | bytes 6311940 | tf_op jit(solution)/shard_map/dot_general | solution.py:49
  134.8 0.6 fusion.157
  136.7 69.3 %all-gather = bf16[98304]{0:T(1024)(128)(2,1)S(1)} all-gather(bf16[3072]{0:T(1024)(128)(2,1)S(1)} %multiply_convert_fusion.1), channel_id=2, replica_groups=mesh['dp'=8,'fsdp'=4] {'dp','fsdp'}, dimensions={0}, use_global_device_ids=true | all-gather | bytes 202752 | tf_op jit(solution)/shard_map/all_gather | solution.py:157
  206.2 0.2 multiply_reduce_fusion.1
  206.4 1.9 fusion.121
  208.3 0.7 subtract_divide_fusion
  209.1 6.5 %fusion.165 = f32[32,1536]{1,0:T(8,128)S(1)} fusion(bf16[32,3072]{1,0:T(8,128)(2,1)S(1)} %reshape.341, bf16[1536,3072]{1,0:T(8,128)(2,1)} %param.27), kind=kOutput, calls=%fused_computation.273 | convolution fusion | flops 301989888 | bytes 9830400 | tf_op jit(solution)/shard_map/dot_general | solution.py:158
  215.6 0.9 copy.44
  216.5 4.0 %fusion = bf16[2048,1536]{1,0:T(8,128)(2,1)S(1)} fusion(bf16[2048,1536]{1,0:T(8,128)(2,1)} %all-gather.7.cloned.1.call-done, f32[32,1536]{1,0:T(8,128)S(1)} %fusion.165), kind=kLoop, calls=%fused_computation.49 | loop fusion | flops 9437184 | bytes 12779520 | tf_op jit(solution)/shard_map/convert_element_type | solution.py:164
  220.5 4.1 %fusion.166 = f32[384,1536]{1,0:T(8,128)} fusion(bf16[2048,384]{1,0:T(8,128)(2,1)S(1)} %bitcast.105, bf16[2048,1536]{1,0:T(8,128)(2,1)S(1)} %fusion), kind=kOutput, calls=%fused_computation.274 | convolution fusion | flops 2415919104 | bytes 10223616 | tf_op jit(solution)/shard_map/dot_general | solution.py:167
  (69 shorter events, 1.2 us)
Async XLA Ops:
  8.0 55.4 %all-gather.5.cloned.1.call-start = ((), (), s32[]{:S(2)}) async-start(), calls=%async_computation.3 | async-start | bytes 1966080 | tf_op jit(solution)/shard_map/all_gather | solution.py:119
  14.6 6.0 %copy-start.10 = (f32[3072]{0:T(1024)S(1)}, f32[3072]{0:T(1024)}, u32[]{:S(2)}) copy-start(f32[3072]{0:T(1024)} %param.25) | copy-start | bytes 36868
  14.6 6.0 %copy-start.11 = (f32[3072]{0:T(1024)S(1)}, f32[3072]{0:T(1024)}, u32[]{:S(2)}) copy-start(f32[3072]{0:T(1024)} %param.24) | copy-start | bytes 36868
  20.1 2.8 %copy-start.2 = (bf16[32,1024]{1,0:T(8,128)(2,1)S(1)}, bf16[32,1024]{1,0:T(8,128)(2,1)}, u32[]{:S(2)}) copy-start(bf16[32,1024]{1,0:T(8,128)(2,1)} %param.16) | copy-start | bytes 196612
  20.1 2.9 %copy-start.13 = (s32[32]{0:T(128)S(1)}, s32[32]{0:T(128)}, u32[]{:S(2)}) copy-start(s32[32]{0:T(128)} %param.18) | copy-start | bytes 388
  20.1 2.9 %copy-start.14 = (s32[32]{0:T(128)S(1)}, s32[32]{0:T(128)}, u32[]{:S(2)}) copy-start(s32[32]{0:T(128)} %param.19) | copy-start | bytes 388
  20.2 21.0 %copy-start.4 = (bf16[32,1024]{1,0:T(8,128)(2,1)S(1)}, bf16[32,1024]{1,0:T(8,128)(2,1)}, u32[]{:S(2)}) copy-start(bf16[32,1024]{1,0:T(8,128)(2,1)} %param.17) | copy-start | bytes 196612
  21.5 66.4 %reduce-scatter.5.cloned.1.call-start = ((), (), s32[]{:S(2)}) async-start(), calls=%async_computation.5 | async-start | bytes 589824 | tf_op jit(solution)/shard_map/reduce_scatter | solution.py:179
  53.2 67.3 %reduce-scatter.3.cloned.1.call-start = ((), (), s32[]{:S(2)}) async-start(), calls=%async_computation.4 | async-start | bytes 491520 | tf_op jit(solution)/shard_map/reduce_scatter | solution.py:148
  69.4 0.6 copy-start.6
  76.0 140.6 %all-gather.7.cloned.1.call-start = ((), (), s32[]{:S(2)}) async-start(), calls=%async_computation.6 | async-start | bytes 7077888 | tf_op jit(solution)/shard_map/all_gather | solution.py:151
  76.0 1.9 copy-start.1
  76.0 14.6 %copy-start = (bf16[256,3072]{1,0:T(8,128)(2,1)S(1)}, bf16[256,3072]{1,0:T(8,128)(2,1)}, u32[]{:S(2)}) copy-start(bf16[256,3072]{1,0:T(8,128)(2,1)} %all-gather.5.cloned.1.call-done) | copy-start | bytes 4718596
  92.2 3.7 %copy-start.7 = (f32[4,1536]{1,0:T(4,128)S(1)}, f32[4,1536]{1,0:T(4,128)}, u32[]{:S(2)}) copy-start(f32[4,1536]{1,0:T(4,128)} %copy-done.6) | copy-start | bytes 73732
  92.2 29.1 %copy-start.9 = (f32[3072]{0:T(1024)S(1)}, f32[3072]{0:T(1024)}, u32[]{:S(2)}) copy-start(f32[3072]{0:T(1024)} %param.28) | copy-start | bytes 36868
  92.2 31.6 %copy-start.8 = (f32[3072]{0:T(1024)S(1)}, f32[3072]{0:T(1024)}, u32[]{:S(2)}) copy-start(f32[3072]{0:T(1024)} %param.29) | copy-start | bytes 36868
  92.2 31.6 %copy-start.12 = (f32[3072]{0:T(1024)S(1)}, f32[3072]{0:T(1024)}, u32[]{:S(2)}) copy-start(f32[3072]{0:T(1024)} %param.30) | copy-start | bytes 36868
  92.2 123.4 %all-to-all-start = ((bf16[256,8,384]{0,2,1:T(8,128)(2,1)}), bf16[256,8,384]{0,2,1:T(8,128)(2,1)S(1)}, u32[]{:S(2)}, u32[]{:S(2)}) async-start(bf16[256,8,384]{0,2,1:T(8,128)(2,1)} %bitcast.61), calls=%async_computation.2 | async-start | bytes 3145728 | tf_op jit(solution)/shard_map/all_to_all | solution.py:152
  123.9 5.1 %copy-start.5 = (bf16[48,1024]{1,0:T(8,128)(2,1)S(1)}, bf16[48,1024]{1,0:T(8,128)(2,1)}, u32[]{:S(2)}) copy-start(bf16[48,1024]{1,0:T(8,128)(2,1)} %reduce-scatter.3.cloned.1.call-done) | copy-start | bytes 294916
  130.2 76.0 %copy-start.3 = (bf16[32,1024]{1,0:T(8,128)(2,1)S(1)}, bf16[32,1024]{1,0:T(8,128)(2,1)}, u32[]{:S(2)}) copy-start(bf16[32,1024]{1,0:T(8,128)(2,1)} %param.16) | copy-start | bytes 196612
Sparse Core Ops, SparseCore 0:
  21.7 41.7 all-gather.4
Sparse Core Ops, SparseCore 1:
  53.3 34.5 reduce-scatter.4
  90.1 20.9 reduce-scatter.2
  112.7 43.7 all-gather.6
where the time goes:
time: 233 us; the launch traced here: 232 us
  blocking collectives  121 us (52%)
  matrix products  33.5 us (14%)
  other arithmetic  22.5 us (10%)
  between operations  20.8 us (9%)
  waiting for transfers between devices  19.8 us (8%)
  local copies, waits for them, and re-layouts  10.3 us (4%)
  starting transfers between devices  3.9 us (2%)
    all_gather x1, blocking collectives, on_device(): all_grad = lax.all_gather(grad_row, ('dp', 'fsdp'), axis=0, tiled=True)  69.3 us
    all_gather x1, blocking collectives, on_device(): all_active = lax.all_gather(active_total, 'dp', axis=0, tiled=True)  24.4 us
    all_gather x1, blocking collectives, on_device(): group_img = lax.all_gather(img_b, 'fsdp', axis=0, tiled=True)  17.6 us
    all_gather x1, blocking collectives, on_device(): column_txt = lax.all_gather(txt_b, 'dp', axis=0, tiled=True)  10.1 us
    reduce_scatter x1, waiting for transfers between devices, on_device(): lax.psum_scatter(text_part.astype(jnp.bfloat16), 'dp', scatter_dimension=...  9.87 us
    all_gather x1, waiting for transfers between devices, on_device(): group_normed = lax.all_gather(normed, 'fsdp', axis=0, tiled=True)  9.79 us
    dot_general x1, matrix products, on_device(): row_down = jnp.dot(all_grad, w_down.T, preferred_element_type=jnp.float32)  6.54 us
    reduce_sum x2, other arithmetic, layer_norm(): centre = jnp.mean(values, axis=-1, keepdims=True)  6.11 us
  transfers between devices with their start and end apart: 5, of which 2 were waited for; matrix products, arithmetic and copies ran while one was open for 19% of the time, Pallas kernels for 0%

commit v1 on v0

--- a/solution.py
+++ b/solution.py
@@ -5,6 +5,29 @@
 
 KERNEL = 7
 SIDE = 8
+
+
+def replace_blocks(inner_x, ndim_at):
+    inner_x = jnp.moveaxis(inner_x, 0, ndim_at)
+    state_next = inner_x.shape
+    return inner_x.reshape(
+        *state_next[:ndim_at],
+        state_next[ndim_at] * state_next[ndim_at + 1],
+        *state_next[ndim_at + 2 :]
+    )
+
+
+def targets_perform(local_block, shard_axis):
+    dev_n = lax.axis_size(shard_axis)
+    w1 = local_block[None]
+    for nth in range(dev_n.bit_length() - 1):
+        h_now = 1 << nth
+        top = lax.ppermute(w1, shard_axis, [(hop_no, hop_no ^ h_now) for hop_no in range(dev_n)])
+        field_out = jnp.stack([w1, top])
+        e_next = lax.axis_index(shard_axis)
+        far_arr = e_next >> nth & 1
+        w1 = jnp.where(far_arr == 0, field_out, field_out[::-1]).reshape(-1, *local_block.shape)
+    return w1
 
 
 def unit_rows(matrix):
@@ -154,7 +177,12 @@
     grad_row = head_back(
         patch_means, block_mean, image_sum[:1], layer_scale, head_gain, head_bias, w_proj
     )
-    all_grad = lax.all_gather(grad_row, ("dp", "fsdp"), axis=0, tiled=True)
+
+    def guide_side(arr_in, mat, k_dim=0):
+        reached = targets_perform(arr_in, mat)
+        return replace_blocks(reached, k_dim)
+
+    all_grad = guide_side(grad_row, ("dp", "fsdp"))
     row_down = jnp.dot(all_grad, w_down.T, preferred_element_type=jnp.float32)
     hid_grad = (
         (

time: 233 us -> 211 us (0.906)
  blocking collectives: 121 us -> 66.5 us
  waiting for transfers between devices: 19.8 us -> 50.2 us
  starting transfers between devices: 3.9 us -> 7.04 us
    all_gather x1 -> x0, blocking collectives: 69.3 us -> none  [on_device(): all_grad = lax.all_gather(grad_row, ('dp', 'fsdp'), axis=0, tiled=True)]
    reduce_scatter x1, waiting for transfers between devices: 0.03 us -> 22.6 us  [on_device(): lax.psum_scatter(terms, 'fsdp', scatter_dimension=0, tiled=True)]
    all_gather x1, blocking collectives: 24.4 us -> 38.8 us  [on_device(): all_active = lax.all_gather(active_total, 'dp', axis=0, tiled=True)]
    ppermute x0 -> x5, waiting for transfers between devices: none -> 7.46 us  [targets_perform(): lax.ppermute(w1, shard_axis, [(hop_no, hop_no ^ h_now) for hop_no in rang...]
    ppermute x0 -> x5, starting transfers between devices: none -> 3.05 us  [targets_perform(): lax.ppermute(w1, shard_axis, [(hop_no, hop_no ^ h_now) for hop_no in rang...]
  transfers between devices with their start and end apart: 5 -> 10, of which waited for: 2 -> 6; matrix products, arithmetic and copies ran while one was open for 19% -> 21% of each run, Pallas kernels for 0% -> 0%
where the time goes in v1:
time: 211 us; the launch traced here: 210 us
  blocking collectives  66.5 us (32%)
  waiting for transfers between devices  50.2 us (24%)
  matrix products  33.5 us (16%)
  other arithmetic  21.9 us (10%)
  between operations  20.9 us (10%)
  local copies, waits for them, and re-layouts  10.4 us (5%)
  starting transfers between devices  7.04 us (3%)
    all_gather x1, blocking collectives, on_device(): all_active = lax.all_gather(active_total, 'dp', axis=0, tiled=True)  38.8 us
    reduce_scatter x1, waiting for transfers between devices, on_device(): lax.psum_scatter(terms, 'fsdp', scatter_dimension=0, tiled=True)  22.6 us
    all_gather x1, blocking collectives, on_device(): group_img = lax.all_gather(img_b, 'fsdp', axis=0, tiled=True)  17.6 us
    reduce_scatter x1, waiting for transfers between devices, on_device(): lax.psum_scatter(text_part.astype(jnp.bfloat16), 'dp', scatter_dimension=...  10.2 us
    all_gather x1, blocking collectives, on_device(): column_txt = lax.all_gather(txt_b, 'dp', axis=0, tiled=True)  10.1 us
    all_gather x1, waiting for transfers between devices, on_device(): group_normed = lax.all_gather(normed, 'fsdp', axis=0, tiled=True)  9.79 us
    ppermute x5, waiting for transfers between devices, targets_perform(): lax.ppermute(w1, shard_axis, [(hop_no, hop_no ^ h_now) for hop_no in rang...  7.46 us
    dot_general x1, matrix products, on_device(): row_down = jnp.dot(all_grad, w_down.T, preferred_element_type=jnp.float32)  6.54 us
  transfers between devices with their start and end apart: 10, of which 6 were waited for; matrix products, arithmetic and copies ran while one was open for 21% of the time, Pallas kernels for 0%

profile of v1, /device:TPU:0, one launch (start us, length us, event | category | flops | bytes accessed | tf_op | source)
XLA Modules:
  0.0 210.4 jit_solution(273732408413479940)
XLA Ops:
  8.0 1.5 fusion.167
  9.5 2.1 fusion.165
  11.6 1.9 fusion.166
  13.5 1.1 convert_bitcast_fusion
  14.6 5.5 %fusion.163 = (f32[8,8]{1,0:T(8,128)S(1)}, f32[1,8,8,3072]{3,2,1,0:T(8,128)S(1)}) fusion(f32[3072]{0:T(1024)S(1)} %bitcast.150, f32[3072]{0:T(1024)S(1)} %bitcast.151, f32[3072]{0:T(1024)S(1)} %bitcast.154, f32[3072]{0:T(1024)S(1)} %bitcast.155, f32[3072]{0:T(1024)S(1)} %bitcast.156, f32[3072]{0:T(1024)S(1)} %bitcast.157, f32[3072]{0:T(1024)S(1)} %bitcast.158, ...), kind=kLoop, calls=%fused_computation.282 | loop fusion | flops 19267520 | bytes 2175232 | tf_op jit(solution)/shard_map/reduce_sum | solution.py:59
  20.2 0.2 multiply_reduce_fusion
  20.6 0.9 fusion.115
  23.5 17.6 %all_gather.15 = bf16[128,1152]{1,0:T(8,128)(2,1)S(1)} all-gather(bf16[32,1152]{1,0:T(8,128)(2,1)S(1)} %fusion.133), channel_id=1, replica_groups=mesh['dp'=8,'fsdp'=4] {'fsdp'}, dimensions={0}, use_global_device_ids=true | all-gather | bytes 368640 | tf_op jit(solution)/shard_map/all_gather | solution.py:136
  41.5 10.1 %all_gather.16 = bf16[256,1152]{1,0:T(8,128)(2,1)S(1)} all-gather(bf16[32,1152]{1,0:T(8,128)(2,1)S(1)} %fusion.134), channel_id=1, replica_groups=mesh['dp'=8,'fsdp'=4] {'dp'}, dimensions={0}, use_global_device_ids=true | all-gather | bytes 663552 | tf_op jit(solution)/shard_map/all_gather | solution.py:137
  51.8 0.3 fusion.15
  52.1 1.1 convolution_convert_fusion
  53.3 0.2 convolution_convert_fusion.1
  53.6 9.8 %all-gather.4.cloned.1.call-done = bf16[256,3072]{1,0:T(8,128)(2,1)} async-done(((bf16[64,3072]{1,0:T(8,128)(2,1)}), bf16[256,3072]{1,0:T(8,128)(2,1)}) %all-gather.4.cloned.1.call-update) | async-done | bytes 1572880 | tf_op jit(solution)/shard_map/all_gather | solution.py:142
  63.4 6.0 %convert_reduce_fusion = (f32[4,1536]{1,0:T(4,128)S(1)}, f32[256,1536]{1,0:T(8,128)S(1)}) fusion(bf16[256,3072]{1,0:T(8,128)(2,1)} %all-gather.4.cloned.1.call-done, bf16[3072,1536]{1,0:T(8,128)(2,1)} %param.26), kind=kOutput, calls=%fused_computation.59 | convolution fusion | flops 2420238336 | bytes 12607488 | tf_op jit(solution)/shard_map/dot_general | solution.py:151
  69.4 5.0 %fusion.140 = f32[8,3072]{1,0:T(8,128)S(1)} fusion(bf16[1536,3072]{1,0:T(8,128)(2,1)} %param.27, bf16[4,1536]{1,0:T(4,128)(2,1)S(1)} %get-tuple-element.71, bf16[4,1536]{1,0:T(4,128)(2,1)S(1)} %get-tuple-element.70), kind=kOutput, calls=%fused_computation.226 | convolution fusion | flops 75546624 | bytes 9560064 | tf_op jit(solution)/shard_map/dot_general | solution.py:159
  74.5 0.9 maximum_maximum_fusion
  75.4 0.2 all-gather.6.cloned.1.call-start
  75.6 1.9 fusion.7
  77.7 10.2 %reduce-scatter.5.cloned.1.call-done = bf16[32,1024]{1,0:T(8,128)(2,1)} async-done(((bf16[256,1024]{1,0:T(8,128)(2,1)}), bf16[32,1024]{1,0:T(8,128)(2,1)}) %reduce-scatter.5.cloned.1.call-update) | async-done | bytes 65552 | tf_op jit(solution)/shard_map/reduce_scatter | solution.py:207
  87.9 1.0 fusion.129
  88.9 22.6 %reduce-scatter.3.cloned.1.call-done = bf16[48,1024]{1,0:T(8,128)(2,1)} async-done(((bf16[192,1024]{1,0:T(8,128)(2,1)}), bf16[48,1024]{1,0:T(8,128)(2,1)}) %reduce-scatter.3.cloned.1.call-update) | async-done | bytes 98320 | tf_op jit(solution)/shard_map/reduce_scatter | solution.py:171
  111.5 0.7 slice.449
  112.3 0.6 fusion.162
  113.5 0.6 multiply_reduce_fusion.3
  114.9 3.7 %fusion.168 = f32[1,1024]{1,0:T(1,128)S(1)} fusion(bf16[3072,1]{0,1:T(2,128)(2,1)S(1)} %reshape.361, bf16[3072,1024]{1,0:T(8,128)(2,1)} %param.31), kind=kOutput, calls=%fused_computation.286 | convolution fusion | flops 6291456 | bytes 6301696 | tf_op jit(solution)/shard_map/dot_general | solution.py:69
  118.6 0.6 multiply_reduce_fusion.5
  120.0 0.6 multiply_reduce_fusion.4
  120.6 0.6 broadcast_multiply_fusion
  121.3 4.6 %fusion.144 = f32[1,3072]{1,0:T(1,128)S(1)} fusion(bf16[3072,1024]{1,0:T(8,128)(2,1)} %param.31, f32[1,1024]{1,0:T(1,128)S(1)} %bitcast.195, f32[48,1024]{1,0:T(8,128)S(1)} %convert_element_type.101, f32[]{:T(128)S(6)} %sqrt.33), kind=kOutput, calls=%fused_computation.240 | convolution fusion | flops 6294528 | bytes 6311940 | tf_op jit(solution)/shard_map/dot_general | solution.py:72
  125.9 0.6 fusion.161
  128.0 0.8 fusion.130
  128.7 1.6 copy.47
  130.3 3.6 %all-to-all-start = ((bf16[256,8,384]{0,2,1:T(8,128)(2,1)}), bf16[256,8,384]{0,2,1:T(8,128)(2,1)S(1)}, u32[]{:S(2)}, u32[]{:S(2)}) async-start(bf16[256,8,384]{0,2,1:T(8,128)(2,1)} %bitcast.61), calls=%async_computation.2 | async-start | bytes 3145728 | tf_op jit(solution)/shard_map/all_to_all | solution.py:175
  134.0 0.6 rev.15
  134.7 1.3 collective-permute-start.1
  136.0 38.8 %all-gather = f32[8,4,1536]{2,1,0:T(4,128)S(1)} all-gather(f32[1,4,1536]{2,1,0:T(4,128)S(1)} %bitcast.135), channel_id=1, replica_groups=mesh['dp'=8,'fsdp'=4] {'dp'}, dimensions={0}, use_global_device_ids=true | all-gather | bytes 221184 | tf_op jit(solution)/shard_map/all_gather | solution.py:176
  175.1 0.4 collective-permute-start.2
  175.5 0.8 collective-permute-done.2
  176.4 0.6 collective-permute-start.3
  177.2 3.3 %collective-permute-done.3 = bf16[8,1,3072]{2,0,1:T(8,128)(2,1)S(1)} collective-permute-done((bf16[8,1,3072]{2,0,1:T(8,128)(2,1)S(1)}, bf16[8,1,3072]{2,0,1:T(8,128)(2,1)S(1)}, u32[]{:S(2)}, u32[]{:S(2)}) %collective-permute-start.3) | collective-permute-done | bytes 49184 | tf_op jit(solution)/shard_map/ppermute | solution.py:25
  180.6 0.6 collective-permute-start.4
  181.2 0.7 subtract_divide_fusion
  182.0 3.3 %collective-permute-done.4 = bf16[16,1,3072]{2,0,1:T(8,128)(2,1)S(1)} collective-permute-done((bf16[16,1,3072]{2,0,1:T(8,128)(2,1)S(1)}, bf16[16,1,3072]{2,0,1:T(8,128)(2,1)S(1)}, u32[]{:S(2)}, u32[]{:S(2)}) %collective-permute-start.4) | collective-permute-done | bytes 98336 | tf_op jit(solution)/shard_map/ppermute | solution.py:25
  185.4 1.9 fusion.121
  187.3 6.5 %fusion.169 = f32[32,1536]{1,0:T(8,128)S(1)} fusion(bf16[32,3072]{1,0:T(8,128)(2,1)S(1)} %bitcast.134, bf16[1536,3072]{1,0:T(8,128)(2,1)} %param.27), kind=kOutput, calls=%fused_computation.287 | convolution fusion | flops 301989888 | bytes 9830400 | tf_op jit(solution)/shard_map/dot_general | solution.py:186
  193.9 0.9 copy.48
  194.8 4.0 %fusion = bf16[2048,1536]{1,0:T(8,128)(2,1)S(1)} fusion(bf16[2048,1536]{1,0:T(8,128)(2,1)} %all-gather.6.cloned.1.call-done, f32[32,1536]{1,0:T(8,128)S(1)} %fusion.169), kind=kLoop, calls=%fused_computation.49 | loop fusion | flops 9437184 | bytes 12779520 | tf_op jit(solution)/shard_map/convert_element_type | solution.py:192
  198.8 4.1 %fusion.170 = f32[384,1536]{1,0:T(8,128)} fusion(bf16[2048,384]{1,0:T(8,128)(2,1)S(1)} %bitcast.129, bf16[2048,1536]{1,0:T(8,128)(2,1)S(1)} %fusion), kind=kOutput, calls=%fused_computation.288 | convolution fusion | flops 2415919104 | bytes 10223616 | tf_op jit(solution)/shard_map/dot_general | solution.py:195
  (90 shorter events, 2.6 us)
Async XLA Ops:
  8.0 55.4 %all-gather.4.cloned.1.call-start = ((), (), s32[]{:S(2)}) async-start(), calls=%async_computation.3 | async-start | bytes 1966080 | tf_op jit(solution)/shard_map/all_gather | solution.py:142
  14.6 6.0 %copy-start.8 = (f32[3072]{0:T(1024)S(1)}, f32[3072]{0:T(1024)}, u32[]{:S(2)}) copy-start(f32[3072]{0:T(1024)} %param.25) | copy-start | bytes 36868
  14.6 6.0 %copy-start.9 = (f32[3072]{0:T(1024)S(1)}, f32[3072]{0:T(1024)}, u32[]{:S(2)}) copy-start(f32[3072]{0:T(1024)} %param.24) | copy-start | bytes 36868
  20.1 2.8 %copy-start.2 = (bf16[32,1024]{1,0:T(8,128)(2,1)S(1)}, bf16[32,1024]{1,0:T(8,128)(2,1)}, u32[]{:S(2)}) copy-start(bf16[32,1024]{1,0:T(8,128)(2,1)} %param.16) | copy-start | bytes 196612
  20.1 2.9 %copy-start.11 = (s32[32]{0:T(128)S(1)}, s32[32]{0:T(128)}, u32[]{:S(2)}) copy-start(s32[32]{0:T(128)} %param.18) | copy-start | bytes 388
  20.1 2.9 %copy-start.12 = (s32[32]{0:T(128)S(1)}, s32[32]{0:T(128)}, u32[]{:S(2)}) copy-start(s32[32]{0:T(128)} %param.19) | copy-start | bytes 388
  20.2 21.0 %copy-start.3 = (bf16[32,1024]{1,0:T(8,128)(2,1)S(1)}, bf16[32,1024]{1,0:T(8,128)(2,1)}, u32[]{:S(2)}) copy-start(bf16[32,1024]{1,0:T(8,128)(2,1)} %param.17) | copy-start | bytes 196612
  21.5 66.4 %reduce-scatter.5.cloned.1.call-start = ((), (), s32[]{:S(2)}) async-start(), calls=%async_computation.5 | async-start | bytes 589824 | tf_op jit(solution)/shard_map/reduce_scatter | solution.py:207
  53.2 58.3 %reduce-scatter.3.cloned.1.call-start = ((), (), s32[]{:S(2)}) async-start(), calls=%async_computation.4 | async-start | bytes 491520 | tf_op jit(solution)/shard_map/reduce_scatter | solution.py:171
  75.4 119.4 %all-gather.6.cloned.1.call-start = ((), (), s32[]{:S(2)}) async-start(), calls=%async_computation.6 | async-start | bytes 7077888 | tf_op jit(solution)/shard_map/all_gather | solution.py:174
  75.6 2.0 copy-start.1
  75.6 36.7 %copy-start.7 = (f32[3072]{0:T(1024)S(1)}, f32[3072]{0:T(1024)}, u32[]{:S(2)}) copy-start(f32[3072]{0:T(1024)} %param.28) | copy-start | bytes 36868
  75.6 39.2 %copy-start.6 = (f32[3072]{0:T(1024)S(1)}, f32[3072]{0:T(1024)}, u32[]{:S(2)}) copy-start(f32[3072]{0:T(1024)} %param.29) | copy-start | bytes 36868
  75.6 39.2 %copy-start.10 = (f32[3072]{0:T(1024)S(1)}, f32[3072]{0:T(1024)}, u32[]{:S(2)}) copy-start(f32[3072]{0:T(1024)} %param.30) | copy-start | bytes 36868
  114.9 5.1 %copy-start.5 = (bf16[48,1024]{1,0:T(8,128)(2,1)S(1)}, bf16[48,1024]{1,0:T(8,128)(2,1)}, u32[]{:S(2)}) copy-start(bf16[48,1024]{1,0:T(8,128)(2,1)} %reduce-scatter.3.cloned.1.call-done) | copy-start | bytes 294916
  121.3 6.7 %copy-start.4 = (bf16[32,1024]{1,0:T(8,128)(2,1)S(1)}, bf16[32,1024]{1,0:T(8,128)(2,1)}, u32[]{:S(2)}) copy-start(bf16[32,1024]{1,0:T(8,128)(2,1)} %reduce-scatter.5.cloned.1.call-done) | copy-start | bytes 196612
  121.3 7.4 %copy-start = (bf16[256,3072]{1,0:T(8,128)(2,1)S(1)}, bf16[256,3072]{1,0:T(8,128)(2,1)}, u32[]{:S(2)}) copy-start(bf16[256,3072]{1,0:T(8,128)(2,1)} %all-gather.4.cloned.1.call-done) | copy-start | bytes 4718596
  127.9 6.1 %collective-permute-start = (bf16[1,1,3072]{2,1,0:T(2,128)(2,1)S(1)}, bf16[1,1,3072]{2,1,0:T(2,128)(2,1)S(1)}, u32[]{:S(2)}, u32[]{:S(2)}) collective-permute-start(bf16[1,1,3072]{2,1,0:T(2,128)(2,1)S(1)} %broadcast_in_dim.15), channel_id=1, source_target_pairs={{0,1},{1,0},{2,3},{3,2},{4,5},{5,4},{6,7},{7,6},{8,9},{9,8},{10,11... | collective-permute-start | bytes 18440 | tf_op jit(solution)/shard_map/ppermute | solution.py:25
  130.3 63.6 %all-to-all-start = ((bf16[256,8,384]{0,2,1:T(8,128)(2,1)}), bf16[256,8,384]{0,2,1:T(8,128)(2,1)S(1)}, u32[]{:S(2)}, u32[]{:S(2)}) async-start(bf16[256,8,384]{0,2,1:T(8,128)(2,1)} %bitcast.61), calls=%async_computation.2 | async-start | bytes 3145728 | tf_op jit(solution)/shard_map/all_to_all | solution.py:175
  134.7 40.3 %collective-permute-start.1 = (bf16[2,1,3072]{2,0,1:T(2,128)(2,1)S(1)}, bf16[2,1,3072]{2,0,1:T(2,128)(2,1)S(1)}, u32[]{:S(2)}, u32[]{:S(2)}) collective-permute-start(bf16[2,1,3072]{2,0,1:T(2,128)(2,1)S(1)} %get-tuple-element.69), channel_id=1, source_target_pairs={{0,2},{1,3},{2,0},{3,1},{4,6},{5,7},{6,4},{7,5},{8,10},{9,11},{10,... | collective-permute-start | bytes 36872 | tf_op jit(solution)/shard_map/ppermute | solution.py:25
  175.1 1.3 collective-permute-start.2
  176.4 4.2 %collective-permute-start.3 = (bf16[8,1,3072]{2,0,1:T(8,128)(2,1)S(1)}, bf16[8,1,3072]{2,0,1:T(8,128)(2,1)S(1)}, u32[]{:S(2)}, u32[]{:S(2)}) collective-permute-start(bf16[8,1,3072]{2,0,1:T(8,128)(2,1)S(1)} %reshape.355), channel_id=1, source_target_pairs={{0,8},{1,9},{2,10},{3,11},{4,12},{5,13},{6,14},{7,15},{8,0},{9,1},... | collective-permute-start | bytes 147464 | tf_op jit(solution)/shard_map/ppermute | solution.py:25
  180.6 4.7 %collective-permute-start.4 = (bf16[16,1,3072]{2,0,1:T(8,128)(2,1)S(1)}, bf16[16,1,3072]{2,0,1:T(8,128)(2,1)S(1)}, u32[]{:S(2)}, u32[]{:S(2)}) collective-permute-start(bf16[16,1,3072]{2,0,1:T(8,128)(2,1)S(1)} %get-tuple-element.67), channel_id=1, source_target_pairs={{0,16},{1,17},{2,18},{3,19},{4,20},{5,21},{6,22},{7,23},{8,24},{9,... | collective-permute-start | bytes 294920 | tf_op jit(solution)/shard_map/ppermute | solution.py:25
Sparse Core Ops, SparseCore 0:
  21.7 41.7 all-gather.3
Sparse Core Ops, SparseCore 1:
  53.3 34.5 reduce-scatter.4
  90.6 20.9 reduce-scatter.2
  113.3 59.4 all-gather.5
